TPU v7x, 32 devices: a whole 2x2x4 slice. The times are simulated.
32 devices in a mesh: blk: 16 (over z, y, core), uly: 2 (over x).
Axes of the slice: x: 2, y: 2, z: 4, core: 2. Of those that a mesh axis runs over, the one named last changes fastest.
Arguments:
- tokens: bfloat16 [4096, 5120], P(('blk', 'uly')), may hold values from -6 to 6
- query_base: bfloat16 [4096, 5120], P(('blk', 'uly')), may hold values from -9 to 9
- key_base: bfloat16 [4096, 5120], P(('blk', 'uly')), may hold values from -9 to 9
- value_base: bfloat16 [4096, 5120], P(('blk', 'uly')), may hold values from -6 to 6
- out_grad: bfloat16 [4096, 5120], P(('blk', 'uly')), may hold values from -0.059814453 to 0.059814453
- down_q: bfloat16 [5120, 64], replicated, may hold values from -0.078125 to 0.078125
- up_q: bfloat16 [64, 5120], replicated, may hold values from -0.75 to 0.75
- down_v: bfloat16 [5120, 64], replicated, may hold values from -0.078125 to 0.078125
- up_v: bfloat16 [64, 5120], replicated, may hold values from -0.75 to 0.75
Outputs:
- attended: bfloat16 [4096, 5120], P(('blk', 'uly'))
- grad_down_q: bfloat16 [5120, 64], replicated
- grad_up_q: bfloat16 [64, 5120], P(None, 'uly')
- grad_down_v: bfloat16 [5120, 64], replicated
- grad_up_v: bfloat16 [64, 5120], P(None, 'uly')
All inputs are finite; a program needn't handle non-finite values.
Results may differ from a plain program's by a relative error of at most 0.025.
Values may be sent and summed in bfloat16 or wider, within the bound.
A program may use at most 128 MiB of HBM per device.

v0:
```python
import jax
import jax.numpy as jnp
from jax import lax
from jax.sharding import PartitionSpec as P

HEAD = 128


def passed_along(block, axis, distance):
    devices = range(lax.axis_size(axis))
    route = [(i - distance, i) for i in devices if i - distance in devices]
    return lax.ppermute(block, axis, route)


def inner(left, right):
    return lax.dot_general(
        left, right, (((0,), (0,)), ((), ())), preferred_element_type=jnp.float32
    )


def head_pass(query, keys, values, upstream, usable, scale):
    scores = jnp.dot(query, keys.T, preferred_element_type=jnp.float32) * scale
    scores = jnp.where(usable[None, :], scores, -jnp.inf)
    top = jnp.max(scores, axis=1, keepdims=True)
    total = jnp.sum(jnp.exp(scores - top), axis=1, keepdims=True)
    probs = jnp.exp(scores - top - jnp.log(total)).astype(jnp.bfloat16)
    attended = jnp.dot(probs, values, preferred_element_type=jnp.float32).astype(jnp.bfloat16)
    delta = jnp.sum(
        upstream.astype(jnp.float32) * attended.astype(jnp.float32), axis=1, keepdims=True
    )
    prob_grad = jnp.dot(upstream, values.T, preferred_element_type=jnp.float32)
    score_grad = (probs.astype(jnp.float32) * (prob_grad - delta)).astype(jnp.bfloat16)
    query_grad = (jnp.dot(score_grad, keys, preferred_element_type=jnp.float32) * scale).astype(
        jnp.bfloat16
    )
    value_terms = jnp.dot(probs.T, upstream, preferred_element_type=jnp.float32)
    return (attended, query_grad, value_terms)


def per_device(tokens, query_base, key_base, value_base, out_grad, down_q, up_q, down_v, up_v):
    low_q = jnp.dot(tokens, down_q, preferred_element_type=jnp.float32).astype(jnp.bfloat16)
    low_v = jnp.dot(tokens, down_v, preferred_element_type=jnp.float32).astype(jnp.bfloat16)
    query = (
        query_base.astype(jnp.float32) + jnp.dot(low_q, up_q, preferred_element_type=jnp.float32)
    ).astype(jnp.bfloat16)
    value = (
        value_base.astype(jnp.float32) + jnp.dot(low_v, up_v, preferred_element_type=jnp.float32)
    ).astype(jnp.bfloat16)
    query_h, keys_h, values_h, upstream_h = (
        lax.all_to_all(query, "uly", split_axis=1, concat_axis=0, tiled=True),
        lax.all_to_all(key_base, "uly", split_axis=1, concat_axis=0, tiled=True),
        lax.all_to_all(value, "uly", split_axis=1, concat_axis=0, tiled=True),
        lax.all_to_all(out_grad, "uly", split_axis=1, concat_axis=0, tiled=True),
    )
    rows = query_h.shape[0]
    width = query_h.shape[1]
    heads_here = width // HEAD
    scale = HEAD ** (-0.5)
    earlier = passed_along(jnp.stack([keys_h, values_h]), "blk", 1)
    keys_all = jnp.concatenate([earlier[0], keys_h], 0)
    values_all = jnp.concatenate([earlier[1], values_h], 0)
    column = jnp.arange(2 * rows)
    usable = jnp.logical_or(column >= rows, lax.axis_index("blk") > 0)

    def per_head(index, carry):
        attended, query_grad, own_terms, prior_terms = carry
        start = index * HEAD
        result = head_pass(
            lax.dynamic_slice_in_dim(query_h, start, HEAD, 1),
            lax.dynamic_slice_in_dim(keys_all, start, HEAD, 1),
            lax.dynamic_slice_in_dim(values_all, start, HEAD, 1),
            lax.dynamic_slice_in_dim(upstream_h, start, HEAD, 1),
            usable,
            scale,
        )
        attended = lax.dynamic_update_slice_in_dim(attended, result[0], start, 1)
        query_grad = lax.dynamic_update_slice_in_dim(query_grad, result[1], start, 1)
        prior_terms = lax.dynamic_update_slice_in_dim(prior_terms, result[2][:rows], start, 1)
        own_terms = lax.dynamic_update_slice_in_dim(own_terms, result[2][rows:], start, 1)
        return (attended, query_grad, own_terms, prior_terms)

    empty_half = jnp.zeros((rows, width), jnp.bfloat16)
    empty_full = jnp.zeros((rows, width), jnp.float32)
    attended_h, query_grad_h, own_terms, prior_terms = lax.fori_loop(
        0, heads_here, per_head, (empty_half, empty_half, empty_full, empty_full)
    )
    returned = passed_along(prior_terms, "blk", -1)
    value_grad_h = (own_terms + returned).astype(jnp.bfloat16)
    rank = down_q.shape[1]
    first_col = lax.axis_index("uly") * width
    attended = lax.all_to_all(attended_h, "uly", split_axis=0, concat_axis=1, tiled=True)
    block_lows = lax.all_gather(jnp.concatenate([low_q, low_v], 1), "uly", axis=0, tiled=True)
    cols_q = lax.dynamic_slice_in_dim(up_q, first_col, width, 1)
    cols_v = lax.dynamic_slice_in_dim(up_v, first_col, width, 1)
    partial_rank = jnp.concatenate(
        [
            jnp.dot(query_grad_h, cols_q.T, preferred_element_type=jnp.float32),
            jnp.dot(value_grad_h, cols_v.T, preferred_element_type=jnp.float32),
        ],
        1,
    )
    lowrank = lax.psum_scatter(partial_rank, "uly", scatter_dimension=0, tiled=True).astype(
        jnp.bfloat16
    )
    down_total = lax.psum(inner(tokens, lowrank), ("blk", "uly"))
    up_q_terms = inner(block_lows[:, :rank], query_grad_h)
    up_v_terms = inner(block_lows[:, rank:], value_grad_h)
    up_q_part, up_v_part = (
        lax.psum(up_q_terms.astype(jnp.bfloat16), "blk").astype(jnp.float32),
        lax.psum(up_v_terms.astype(jnp.bfloat16), "blk").astype(jnp.float32),
    )
    return (
        attended,
        down_total[:, :rank].astype(jnp.bfloat16),
        up_q_part.astype(jnp.bfloat16),
        down_total[:, rank:].astype(jnp.bfloat16),
        up_v_part.astype(jnp.bfloat16),
    )


def solution(mesh):
    return jax.shard_map(
        per_device,
        mesh=mesh,
        in_specs=(
            P(("blk", "uly"), None),
            P(("blk", "uly"), None),
            P(("blk", "uly"), None),
            P(("blk", "uly"), None),
            P(("blk", "uly"), None),
            P(),
            P(),
            P(),
            P(),
        ),
        out_specs=(P(("blk", "uly"), None), P(), P(None, "uly"), P(), P(None, "uly")),
        check_vma=False,
    )
```

profile of v0, /device:TPU:0, one launch (start us, length us, event | category | flops | bytes accessed | tf_op | source)
XLA Modules:
  0.0 393.2 jit_solution(3088520763562678787)
XLA Ops:
  8.0 1.3 copy-done
  9.3 1.7 convolution_convert_fusion.3
  12.7 4.2 %all-to-all-start.2 = ((bf16[128,2,2560]{2,0,1:T(8,128)(2,1)}), bf16[128,2,2560]{2,0,1:T(8,128)(2,1)S(1)}, u32[]{:S(2)}, u32[]{:S(2)}) async-start(bf16[128,2,2560]{2,0,1:T(8,128)(2,1)} %bitcast.73), calls=%async_computation.2 | async-start | bytes 2621440 | tf_op jit(solution)/shard_map/all_to_all | solution.py:52
  16.9 2.5 copy.47
  19.4 14.8 %all-to-all-done.2 = bf16[128,2,2560]{2,0,1:T(8,128)(2,1)S(1)} async-done(((bf16[128,2,2560]{2,0,1:T(8,128)(2,1)}), bf16[128,2,2560]{2,0,1:T(8,128)(2,1)S(1)}, u32[]{:S(2)}, u32[]{:S(2)}) %all-to-all-start.2) | async-done | bytes 1310752 | tf_op jit(solution)/shard_map/all_to_all | solution.py:52
  34.2 19.7 %all_to_all.95 = bf16[128,2,2560]{2,0,1:T(8,128)(2,1)S(1)} all-to-all(bf16[128,2,2560]{2,0,1:T(8,128)(2,1)} %bitcast.74), channel_id=1, replica_groups=mesh['blk'=16,'uly'=2] {'uly'}, dimensions={1} | all-to-all | bytes 2621440 | tf_op jit(solution)/shard_map/all_to_all | solution.py:51
  53.9 1.9 pad_maximum_fusion
  55.8 2.8 collective-permute-start
  58.6 2.5 copy.30
  61.1 4.6 %all-to-all-start.3 = ((bf16[128,2,2560]{0,2,1:T(8,128)(2,1)}), bf16[128,2,2560]{0,2,1:T(8,128)(2,1)}, u32[]{:S(2)}, u32[]{:S(2)}) async-start(bf16[128,2,2560]{0,2,1:T(8,128)(2,1)} %bitcast.71), calls=%async_computation.3 | async-start | bytes 2621440 | tf_op jit(solution)/shard_map/all_to_all | solution.py:53
  69.0 14.5 %all-to-all-done.3 = bf16[128,2,2560]{0,2,1:T(8,128)(2,1)} async-done(((bf16[128,2,2560]{0,2,1:T(8,128)(2,1)}), bf16[128,2,2560]{0,2,1:T(8,128)(2,1)}, u32[]{:S(2)}, u32[]{:S(2)}) %all-to-all-start.3) | async-done | bytes 1310752 | tf_op jit(solution)/shard_map/all_to_all | solution.py:53
  83.4 4.5 %all-to-all-start = ((bf16[128,2,2560]{2,0,1:T(8,128)(2,1)}), bf16[128,2,2560]{2,0,1:T(8,128)(2,1)}, u32[]{:S(2)}, u32[]{:S(2)}) async-start(bf16[128,2,2560]{2,0,1:T(8,128)(2,1)} %bitcast.70), calls=%async_computation | async-start | bytes 2621440 | tf_op jit(solution)/shard_map/all_to_all | solution.py:50
  88.0 2.5 copy.31
  90.4 2.0 slice_bitcast_fusion
  92.5 2.5 pad_maximum_fusion.1
  95.1 9.7 %all-to-all-done = bf16[128,2,2560]{2,0,1:T(8,128)(2,1)} async-done(((bf16[128,2,2560]{2,0,1:T(8,128)(2,1)}), bf16[128,2,2560]{2,0,1:T(8,128)(2,1)}, u32[]{:S(2)}, u32[]{:S(2)}) %all-to-all-start) | async-done | bytes 1310752 | tf_op jit(solution)/shard_map/all_to_all | solution.py:50
  104.8 1.8 broadcast_in_dim.43
  106.5 1.9 broadcast_in_dim.43.clone
  109.6 139.5 %while.20 = (s32[]{:T(128)}, bf16[256,2560]{1,0:T(8,128)(2,1)}, bf16[256,2560]{1,0:T(8,128)(2,1)S(1)}, f32[256,2560]{1,0:T(8,128)}, f32[256,2560]{1,0:T(8,128)},...) while((s32[]{:T(128)}, bf16[256,2560]{1,0:T(8,128)(2,1)}, ...), condition=%wide.region_4.5_spmd.clone, body=%wide.region_0.4_spmd.clone.sunk | while | flops 169574656 | bytes 4862660 | solution.py:84
  109.7 1.3 fusion.70
  114.5 1.4 fusion.71
  116.6 1.3 fusion.70
  121.5 1.4 fusion.71
  123.6 1.3 fusion.70
  128.4 1.4 fusion.71
  135.4 1.4 fusion.71
  137.5 1.3 fusion.70
  142.3 1.4 fusion.71
  144.5 1.3 fusion.70
  149.4 1.4 fusion.71
  151.5 1.3 fusion.70
  156.3 1.4 fusion.71
  158.5 1.3 fusion.70
  163.3 1.4 fusion.71
  170.3 1.4 fusion.71
  172.4 1.3 fusion.70
  177.3 1.4 fusion.71
  179.4 1.3 fusion.70
  184.3 1.4 fusion.71
  191.2 1.4 fusion.71
  193.3 1.3 fusion.70
  198.2 1.4 fusion.71
  205.2 1.4 fusion.71
  212.1 1.4 fusion.71
  214.3 1.3 fusion.70
  219.1 1.4 fusion.71
  226.1 1.4 fusion.71
  228.2 1.3 fusion.70
  233.0 1.4 fusion.71
  240.1 1.4 fusion.71
  242.2 1.3 fusion.70
  247.0 1.4 fusion.71
  249.2 1.3 collective-permute-start.1
  250.5 4.7 %all-to-all-start.4 = ((bf16[2,128,2560]{2,1,0:T(8,128)(2,1)}), bf16[2,128,2560]{2,1,0:T(8,128)(2,1)}, u32[]{:S(2)}, u32[]{:S(2)}) async-start(bf16[2,128,2560]{2,1,0:T(8,128)(2,1)} %bitcast.72), calls=%async_computation.4 | async-start | bytes 2621440 | tf_op jit(solution)/shard_map/all_to_all | solution.py:91
  255.2 18.3 %all_gather.3 = bf16[256,128]{0,1:T(8,128)(2,1)S(1)} all-gather(bf16[128,128]{0,1:T(8,128)(2,1)S(1)} %pad_maximum_fusion.4), channel_id=1, replica_groups=mesh['blk'=16,'uly'=2] {'uly'}, dimensions={0}, use_global_device_ids=true | all-gather | bytes 98304 | tf_op jit(solution)/shard_map/all_gather | solution.py:92
  275.1 1.8 copy.35
  276.9 1.4 copy.36
  278.3 2.9 add_convert_fusion
  283.6 12.9 %reduce-scatter.2.cloned.1.call-done = f32[128,128]{0,1:T(8,128)} async-done(((f32[256,128]{0,1:T(8,128)}), f32[128,128]{0,1:T(8,128)}) %reduce-scatter.2.cloned.1.call-update) | async-done | bytes 65552 | tf_op jit(solution)/shard_map/reduce_scatter | solution.py:102
  296.4 2.8 convolution_bitcast_fusion
  299.3 74.1 %all-reduce.5 = bf16[5120,128]{0,1:T(8,128)(2,1)S(1)} all-reduce(f32[5120,128]{0,1:T(8,128)} %convolution_bitcast_fusion), channel_id=1, replica_groups=mesh['blk'=16,'uly'=2] {'blk','uly'}, use_global_device_ids=true, to_apply=%region_6.7 | all-reduce | flops 655360 | bytes 3932160 | tf_op jit(solution)/shard_map/psum | solution.py:105
  374.5 7.9 %all-reduce.4.cloned.1.call-done = (bf16[64,2560]{1,0:T(8,128)(2,1)}, bf16[64,2560]{1,0:T(8,128)(2,1)}) async-done(((bf16[64,2560]{1,0:T(8,128)(2,1)}, bf16[64,2560]{1,0:T(8,128)(2,1)}), (bf16[64,2560]{1,0:T(8,128)(2,1)}, bf16[64,2560]{1,0:T(8,128)(2,1)})) %all-reduce.4.cloned.1.call-update) | async-done | bytes 655376 | tf_op jit(solution)/shard_map/psum | solution.py:109
  382.4 1.7 copy.76
  384.1 1.7 copy.77
  (267 shorter events, 106.5 us)
Async XLA Ops:
  8.0 1.3 copy-start
  8.0 3.0 copy-start.7
  8.0 3.0 copy-start.5
  12.7 21.5 %all-to-all-start.2 = ((bf16[128,2,2560]{2,0,1:T(8,128)(2,1)}), bf16[128,2,2560]{2,0,1:T(8,128)(2,1)S(1)}, u32[]{:S(2)}, u32[]{:S(2)}) async-start(bf16[128,2,2560]{2,0,1:T(8,128)(2,1)} %bitcast.73), calls=%async_computation.2 | async-start | bytes 2621440 | tf_op jit(solution)/shard_map/all_to_all | solution.py:52
  53.9 1.9 copy-start.1
  55.8 34.6 %collective-permute-start = (bf16[2,256,2560]{2,1,0:T(8,128)(2,1)}, bf16[2,256,2560]{2,1,0:T(8,128)(2,1)}, u32[]{:S(2)}, u32[]{:S(2)}) collective-permute-start(bf16[2,256,2560]{2,1,0:T(8,128)(2,1)} %pad_maximum_fusion), channel_id=1, source_target_pairs={{0,2},{2,4},{4,6},{6,8},{8,10},{10,12},{12,14},{14,16},{16,18},{18... | collective-permute-start | bytes 7864328 | tf_op jit(solution)/shard_map/ppermute | solution.py:12
  61.1 4.7 %copy-start.9 = (bf16[5120,64]{0,1:T(8,128)(2,1)S(1)}, bf16[5120,64]{0,1:T(8,128)(2,1)}, u32[]{:S(2)}) copy-start(bf16[5120,64]{0,1:T(8,128)(2,1)} %param.16) | copy-start | bytes 1966084
  61.1 22.3 %all-to-all-start.3 = ((bf16[128,2,2560]{0,2,1:T(8,128)(2,1)}), bf16[128,2,2560]{0,2,1:T(8,128)(2,1)}, u32[]{:S(2)}, u32[]{:S(2)}) async-start(bf16[128,2,2560]{0,2,1:T(8,128)(2,1)} %bitcast.71), calls=%async_computation.3 | async-start | bytes 2621440 | tf_op jit(solution)/shard_map/all_to_all | solution.py:53
  65.8 1.1 copy-start.3
  65.8 1.5 copy-start.8
  83.4 21.3 %all-to-all-start = ((bf16[128,2,2560]{2,0,1:T(8,128)(2,1)}), bf16[128,2,2560]{2,0,1:T(8,128)(2,1)}, u32[]{:S(2)}, u32[]{:S(2)}) async-start(bf16[128,2,2560]{2,0,1:T(8,128)(2,1)} %bitcast.70), calls=%async_computation | async-start | bytes 2621440 | tf_op jit(solution)/shard_map/all_to_all | solution.py:50
  90.4 2.1 copy-start.2
  249.2 29.1 %collective-permute-start.1 = (f32[256,2560]{1,0:T(8,128)}, f32[256,2560]{1,0:T(8,128)}, u32[]{:S(2)}, u32[]{:S(2)}) collective-permute-start(f32[256,2560]{1,0:T(8,128)} %get-tuple-element.180), channel_id=1, source_target_pairs={{2,0},{4,2},{6,4},{8,6},{10,8},{12,10},{14,12},{16,14},{18,16},{20... | collective-permute-start | bytes 7864328 | tf_op jit(solution)/shard_map/ppermute | solution.py:12
  250.4 23.0 %copy-start.4 = (bf16[64,5120]{1,0:T(8,128)(2,1)S(1)}, bf16[64,5120]{1,0:T(8,128)(2,1)}, u32[]{:S(2)}) copy-start(bf16[64,5120]{1,0:T(8,128)(2,1)} %param.17) | copy-start | bytes 1966084
  250.5 24.6 %all-to-all-start.4 = ((bf16[2,128,2560]{2,1,0:T(8,128)(2,1)}), bf16[2,128,2560]{2,1,0:T(8,128)(2,1)}, u32[]{:S(2)}, u32[]{:S(2)}) async-start(bf16[2,128,2560]{2,1,0:T(8,128)(2,1)} %bitcast.72), calls=%async_computation.4 | async-start | bytes 2621440 | tf_op jit(solution)/shard_map/all_to_all | solution.py:91
  255.1 41.3 %reduce-scatter.2.cloned.1.call-start = ((), (), s32[]{:S(2)}) async-start(), calls=%async_computation.6 | async-start | bytes 196608 | tf_op jit(solution)/shard_map/reduce_scatter | solution.py:102
  278.3 2.9 copy-start.6
  282.4 99.9 %all-reduce.4.cloned.1.call-start = ((), (), s32[]{:S(2)}) async-start(), calls=%async_computation.7 | async-start | bytes 1310720 | tf_op jit(solution)/shard_map/psum | solution.py:109
Sparse Core Ops, SparseCore 0:
  282.5 13.8 reduce-scatter.1
Sparse Core Ops, SparseCore 1:
  286.9 95.4 all-reduce.3
where the time goes:
time: 396 us; the launch traced here: 393 us
  blocking collectives  112 us (28%)
  matrix products  89.7 us (23%)
  local copies, waits for them, and re-layouts  76.7 us (19%)
  waiting for transfers between devices  59.7 us (15%)
  starting transfers between devices  22.2 us (6%)
  other arithmetic  16.2 us (4%)
  between operations  15.7 us (4%)
    psum x1, blocking collectives, per_device(): down_total = lax.psum(inner(tokens, lowrank), ('blk', 'uly'))  74.1 us
    dot_general x20, matrix products, head_pass(): jnp.dot(score_grad, keys, preferred_element_type=jnp.float32) * scale  27.2 us
    dot_general x20, matrix products, head_pass(): scores = jnp.dot(query, keys.T, preferred_element_type=jnp.float32) * scale  25.1 us
    dot_general x20, matrix products, head_pass(): jnp.dot(probs, values, preferred_element_type=jnp.float32)  23.1 us
    all_to_all x1, blocking collectives, per_device(): lax.all_to_all(key_base, 'uly', split_axis=1, concat_axis=0, tiled=True)  19.7 us
    dynamic_slice x40, local copies, waits for them, and re-layouts, per_head(): lax.dynamic_slice_in_dim(upstream_h, start, HEAD, 1)  19.1 us
    all_gather x1, blocking collectives, per_device(): lax.all_gather(jnp.concatenate([low_q, low_v], 1), 'uly', axis=0, tiled=T...  18.3 us
    dynamic_update_slice x20, local copies, waits for them, and re-layouts, per_head(): lax.dynamic_update_slice_in_dim(prior_terms, result[2][:rows], start, 1)  15.6 us
  transfers between devices with their start and end apart: 8, of which 5 were waited for; matrix products, arithmetic and copies ran while one was open for 6% of the time, Pallas kernels for 0%

commit v1 on v0

v1 whole, which is shorter than its diff:
```python
import functools

import jax
import jax.numpy as jnp
from jax import lax
from jax.experimental import pallas as pl
from jax.experimental.pallas import tpu as pltpu
from jax.sharding import PartitionSpec as P

HEAD = 128
CHUNK = 512
MESH = pl.DeviceIdType.MESH
F32 = jnp.float32
BF16 = jnp.bfloat16


def inner(left, right):
    return lax.dot_general(left, right, (((0,), (0,)), ((), ())), preferred_element_type=F32)


def outer(left, right):
    return lax.dot_general(left, right, (((1,), (1,)), ((), ())), preferred_element_type=F32)


def dot(left, right):
    return jnp.dot(left, right, preferred_element_type=F32)


def attention_kernel(
    nb, nu,
    tokens, query_base, key_base, value_base, out_grad, down_q, up_q, down_v, up_v,
    att_ref, gup_ref, low_out,
    kbuf, vbuf, lbuf, tok, qs, gs, dq, dv, ups, lrq, lrv, lrin,
    local_sem, xsend, xrecv, fsend, frecv, lsend, lrecv, msend, mrecv, rsend, rrecv,
):
    blk = lax.axis_index("blk")
    u = lax.axis_index("uly")
    rows, width = tokens.shape
    rank = up_q.shape[0]
    span = nu * rows
    chunks = width // CHUNK
    has_prev = blk > 0
    has_next = blk < nb - 1
    mine = pl.ds(pl.multiple_of(span + u * rows, rows), rows)

    def peer(j):
        return lax.rem(u + j, nu)

    def source(j):
        return lax.rem(u - j + nu, nu)

    def cols(c):
        return pl.ds(pl.multiple_of(c * CHUNK, CHUNK), CHUNK)

    barrier = pltpu.get_barrier_semaphore()
    for j in range(1, nu):
        pl.semaphore_signal(barrier, inc=1, device_id=(blk, peer(j)), device_id_type=MESH)

    @pl.when(has_prev)
    def _():
        for j in range(nu):
            pl.semaphore_signal(barrier, inc=1, device_id=(blk - 1, peer(j)), device_id_type=MESH)

    @pl.when(has_next)
    def _():
        for j in range(nu):
            pl.semaphore_signal(barrier, inc=1, device_id=(blk + 1, peer(j)), device_id_type=MESH)

    local = [
        pltpu.make_async_copy(src, dst, local_sem.at[i])
        for i, (src, dst) in enumerate(
            (
                (tokens, tok), (down_v, dv), (down_q, dq),
                (up_q, ups.at[pl.ds(0, rank)]), (up_v, ups.at[pl.ds(rank, rank)]),
                (value_base, vbuf.at[mine]), (key_base, kbuf.at[mine]),
                (query_base, qs), (out_grad, gs),
            )
        )
    ]
    for copy in local:
        copy.start()

    edge = jnp.logical_or(blk == 0, blk == nb - 1)

    @pl.when(edge)
    def _():
        pl.semaphore_wait(barrier, 2 * nu - 1)

    @pl.when(jnp.logical_not(edge))
    def _():
        pl.semaphore_wait(barrier, 3 * nu - 1)

    bufs = (kbuf, vbuf)

    def across(a, j, c):
        src = key_base.at[:, cols(c)] if a == 0 else vbuf.at[mine, cols(c)]
        return pltpu.make_async_remote_copy(
            src_ref=src, dst_ref=bufs[a].at[mine, cols(c)],
            send_sem=xsend.at[a, j, c], recv_sem=xrecv.at[a, j, c],
            device_id=(blk, peer(j)), device_id_type=MESH,
        )

    def crossed(a, j, c):
        here = bufs[a].at[pl.ds(pl.multiple_of(span + source(j) * rows, rows), rows), cols(c)]
        return pltpu.make_async_remote_copy(
            src_ref=here, dst_ref=here,
            send_sem=xsend.at[a, j, c], recv_sem=xrecv.at[a, j, c],
            device_id=(blk, peer(j)), device_id_type=MESH,
        )

    def onward(a, j, c):
        s = source(j)
        if a == 0 and j == 0:
            src = key_base.at[:, cols(c)]
        else:
            src = bufs[a].at[pl.ds(pl.multiple_of(span + s * rows, rows), rows), cols(c)]
        return pltpu.make_async_remote_copy(
            src_ref=src, dst_ref=bufs[a].at[pl.ds(pl.multiple_of(s * rows, rows), rows), cols(c)],
            send_sem=fsend.at[a, j, c], recv_sem=frecv.at[a, j, c],
            device_id=(blk + 1, u), device_id_type=MESH,
        )

    def arrived(a, j, c):
        here = bufs[a].at[pl.ds(pl.multiple_of(source(j) * rows, rows), rows), cols(c)]
        return pltpu.make_async_remote_copy(
            src_ref=here, dst_ref=here,
            send_sem=fsend.at[a, j, c], recv_sem=frecv.at[a, j, c],
            device_id=(blk, peer(1)), device_id_type=MESH,
        )

    def low_across(j):
        return pltpu.make_async_remote_copy(
            src_ref=lbuf.at[mine], dst_ref=lbuf.at[mine],
            send_sem=lsend.at[j], recv_sem=lrecv.at[j],
            device_id=(blk, peer(j)), device_id_type=MESH,
        )

    def low_crossed(j):
        here = lbuf.at[pl.ds(pl.multiple_of(span + source(j) * rows, rows), rows)]
        return pltpu.make_async_remote_copy(
            src_ref=here, dst_ref=here, send_sem=lsend.at[j], recv_sem=lrecv.at[j],
            device_id=(blk, peer(j)), device_id_type=MESH,
        )

    def low_onward(j):
        s = source(j)
        return pltpu.make_async_remote_copy(
            src_ref=lbuf.at[pl.ds(pl.multiple_of(span + s * rows, rows), rows)],
            dst_ref=lbuf.at[pl.ds(pl.multiple_of(s * rows, rows), rows)],
            send_sem=msend.at[j], recv_sem=mrecv.at[j],
            device_id=(blk + 1, u), device_id_type=MESH,
        )

    def low_arrived(j):
        here = lbuf.at[pl.ds(pl.multiple_of(source(j) * rows, rows), rows)]
        return pltpu.make_async_remote_copy(
            src_ref=here, dst_ref=here, send_sem=msend.at[j], recv_sem=mrecv.at[j],
            device_id=(blk, peer(1)), device_id_type=MESH,
        )

    early = min(3, chunks)
    for c in range(early):
        for j in range(1, nu):
            across(0, j, c).start()

        @pl.when(has_next)
        def _():
            onward(0, 0, c).start()

    lane = lax.broadcasted_iota(jnp.int32, (rows, 2 * rank), 1)
    for i in range(3):
        local[i].wait()
    low = jnp.concatenate([dot(tok[...], dq[...]), dot(tok[...], dv[...])], axis=1)
    low_qm = jnp.where(lane < rank, low, 0.0).astype(BF16)
    low_vm = jnp.where(lane >= rank, low, 0.0).astype(BF16)
    lbuf[mine, :] = low_vm
    for i in range(3, 6):
        local[i].wait()

    @pl.loop(0, chunks)
    def _(c):
        part = dot(low_vm, ups[:, cols(c)])
        vbuf[mine, cols(c)] = (vbuf[mine, cols(c)].astype(F32) + part).astype(BF16)

    for j in range(1, nu):
        low_across(j).start()

    @pl.when(has_next)
    def _():
        low_onward(0).start()

    @pl.loop(0, chunks)
    def _(c):
        @pl.when(c >= early)
        def _():
            for j in range(1, nu):
                across(0, j, c).start()

            @pl.when(has_next)
            def _():
                onward(0, 0, c).start()

        for j in range(1, nu):
            across(1, j, c).start()

        @pl.when(has_next)
        def _():
            onward(1, 0, c).start()

    lrq[...] = jnp.zeros_like(lrq)
    lrv[...] = jnp.zeros_like(lrv)

    @pl.when(jnp.logical_not(has_prev))
    def _():
        kbuf[pl.ds(0, span), :] = jnp.zeros((span, width), BF16)
        vbuf[pl.ds(0, span), :] = jnp.zeros((span, width), BF16)
        lbuf[pl.ds(0, span), :] = jnp.zeros((span, 2 * rank), BF16)

    for i in range(6, 9):
        local[i].wait()

    scale = HEAD ** (-0.5)
    key_at = lax.broadcasted_iota(jnp.int32, (rows, 2 * span), 1)
    usable = jnp.logical_or(key_at >= span, has_prev)

    def head(h):
        at = pl.ds(pl.multiple_of(h * HEAD, HEAD), HEAD)
        up = ups[:, at]
        keys = kbuf[:, at]
        values = vbuf[:, at]
        grad = gs[:, at]
        query = (qs[:, at].astype(F32) + dot(low_qm, up)).astype(BF16)
        scores = jnp.where(usable, outer(query, keys) * scale, -jnp.inf)
        weights = jnp.exp(scores - jnp.max(scores, axis=1, keepdims=True))
        total = jnp.sum(weights, axis=1, keepdims=True)
        probs = (weights * (1.0 / total)).astype(BF16)
        attended = dot(probs, values).astype(BF16)
        att_ref[:, at] = attended
        delta = jnp.sum(grad.astype(F32) * attended.astype(F32), axis=1, keepdims=True)
        score_grad = (probs.astype(F32) * (outer(grad, values) - delta)).astype(BF16)
        query_grad = (dot(score_grad, keys) * scale).astype(BF16)
        seen = dot(probs, lbuf[...]).astype(BF16)
        gup_ref[:, at] = (inner(low_qm, query_grad) + inner(seen, grad)).astype(BF16)
        lrq[...] += jnp.where(lane < rank, outer(query_grad, up), 0.0)
        lifted = jnp.where(lane >= rank, outer(grad, up), 0.0).astype(BF16)
        lrv[...] += inner(probs, lifted)

    heads = CHUNK // HEAD

    @pl.loop(0, chunks + 1)
    def _(c):
        @pl.when(c == 0)
        def _():
            for j in range(1, nu):
                low_crossed(j).wait_recv()

                @pl.when(has_next)
                def _():
                    low_onward(j).start()

            @pl.when(has_prev)
            def _():
                for j in range(nu):
                    low_arrived(j).wait_recv()

        @pl.when(c < chunks)
        def _():
            for a in range(2):
                for j in range(1, nu):
                    crossed(a, j, c).wait_recv()

                    @pl.when(has_next)
                    def _():
                        onward(a, j, c).start()

        @pl.when(c > 0)
        def _():
            @pl.when(has_prev)
            def _():
                for a in range(2):
                    for j in range(nu):
                        arrived(a, j, c - 1).wait_recv()

            @pl.loop(0, heads)
            def _(i):
                head((c - 1) * heads + i)

    def terms(k, j, base):
        s = peer(j)
        return pltpu.make_async_remote_copy(
            src_ref=lrv.at[pl.ds(pl.multiple_of(base + s * rows, rows), rows)],
            dst_ref=lrin.at[k, j],
            send_sem=rsend.at[k, j], recv_sem=rrecv.at[k, j],
            device_id=(blk - k, s), device_id_type=MESH,
        )

    for j in range(1, nu):
        terms(0, j, span).start()

    @pl.when(has_prev)
    def _():
        for j in range(nu):
            terms(1, j, 0).start()

    @pl.loop(0, chunks)
    def _(c):
        for a in range(2):
            for j in range(1, nu):
                across(a, j, c).wait_send()

            @pl.when(has_next)
            def _():
                for j in range(nu):
                    onward(a, j, c).wait_send()

    for j in range(1, nu):
        low_across(j).wait_send()

    @pl.when(has_next)
    def _():
        for j in range(nu):
            low_onward(j).wait_send()

    lrq[...] += lrv[mine, :]
    for j in range(1, nu):
        terms(0, j, span).wait_recv()
        lrq[...] += lrin[0, j]

    @pl.when(has_next)
    def _():
        for j in range(nu):
            terms(1, j, 0).wait_recv()
            lrq[...] += lrin[1, j]

    low_out[...] = lrq[...].astype(BF16)
    for j in range(1, nu):
        terms(0, j, span).wait_send()

    @pl.when(has_prev)
    def _():
        for j in range(nu):
            terms(1, j, 0).wait_send()


def attention(nb, nu, *operands):
    rows, width = operands[0].shape
    rank = operands[6].shape[0]
    span = nu * rows
    chunks = width // CHUNK
    dma = pltpu.SemaphoreType.DMA
    anywhere = pl.BlockSpec(memory_space=pl.ANY)
    here = pl.BlockSpec(memory_space=pltpu.VMEM)
    return pl.pallas_call(
        functools.partial(attention_kernel, nb, nu),
        out_shape=(
            jax.ShapeDtypeStruct((rows, width), BF16),
            jax.ShapeDtypeStruct((2 * rank, width), BF16),
            jax.ShapeDtypeStruct((rows, 2 * rank), BF16),
        ),
        in_specs=[anywhere] * 9,
        out_specs=(here, here, here),
        scratch_shapes=[
            pltpu.VMEM((2 * span, width), BF16),
            pltpu.VMEM((2 * span, width), BF16),
            pltpu.VMEM((2 * span, 2 * rank), BF16),
            pltpu.VMEM((rows, width), BF16),
            pltpu.VMEM((rows, width), BF16),
            pltpu.VMEM((rows, width), BF16),
            pltpu.VMEM((width, rank), BF16),
            pltpu.VMEM((width, rank), BF16),
            pltpu.VMEM((2 * rank, width), BF16),
            pltpu.VMEM((rows, 2 * rank), F32),
            pltpu.VMEM((2 * span, 2 * rank), F32),
            pltpu.VMEM((2, nu, rows, 2 * rank), F32),
            dma((9,)),
            dma((2, nu, chunks)), dma((2, nu, chunks)),
            dma((2, nu, chunks)), dma((2, nu, chunks)),
            dma((nu,)), dma((nu,)), dma((nu,)), dma((nu,)),
            dma((2, nu)), dma((2, nu)),
        ],
        compiler_params=pltpu.CompilerParams(
            collective_id=0, has_side_effects=True, vmem_limit_bytes=65_000_000
        ),
    )(*operands)


def per_device(nb, nu, tokens, query_base, key_base, value_base, out_grad, down_q, up_q, down_v, up_v):
    rank = down_q.shape[1]
    attended, gup, lowrank = attention(
        nb, nu, tokens, query_base, key_base, value_base, out_grad, down_q, up_q, down_v, up_v
    )
    down_total = lax.psum(inner(tokens, lowrank).astype(BF16), ("blk", "uly"))
    gup = lax.psum_scatter(gup, "uly", scatter_dimension=1, tiled=True)
    gup = lax.psum(gup, "blk")
    return (
        attended,
        down_total[:, :rank],
        gup[:rank],
        down_total[:, rank:],
        gup[rank:],
    )


def solution(mesh):
    split = P(("blk", "uly"), None)
    return jax.shard_map(
        functools.partial(per_device, mesh.shape["blk"], mesh.shape["uly"]),
        mesh=mesh,
        in_specs=(split,) * 5 + (P(),) * 4,
        out_specs=(split, P(), P(None, "uly"), P(), P(None, "uly")),
        check_vma=False,
    )
```

time: 396 us -> 354 us (0.89)
  waiting for transfers between devices: 59.7 us -> 246 us
  blocking collectives: 112 us -> 0 us
  matrix products: 89.7 us -> 2.34 us
  Pallas kernels: 0 us -> 78.9 us
  local copies, waits for them, and re-layouts: 76.7 us -> 10.4 us
  starting transfers between devices: 22.2 us -> 0.13 us
  other arithmetic: 16.2 us -> 0 us
    psum x1 -> x2, waiting for transfers between devices: 7.86 us -> 213 us  [the longest x1 122 us: per_device(): down_total = lax.psum(inner(tokens, lowrank).astype(BF16), ('blk', 'uly'))]
    dot_general x86 -> x0, matrix products: 84.7 us -> none  [the longest x20 27.2 us: head_pass(): jnp.dot(score_grad, keys, preferred_element_type=jnp.float32) * scale]
    pallas_call x0 -> x1, Pallas kernels: none -> 78.9 us  [attention(): pl.pallas_call(functools.partial(attention_kernel, nb, nu), out_shape=(ja...]
    psum x1 -> x0, blocking collectives: 74.1 us -> none  [per_device(): down_total = lax.psum(inner(tokens, lowrank), ('blk', 'uly'))]
    all_to_all x4 -> x0, waiting for transfers between devices: 39 us -> none  [the longest x1 14.8 us: per_device(): lax.all_to_all(value, 'uly', split_axis=1, concat_axis=0, tiled=True)]
    dynamic_update_slice x60 -> x0, local copies, waits for them, and re-layouts: 30.7 us -> none  [the longest x20 15.6 us: per_head(): lax.dynamic_update_slice_in_dim(prior_terms, result[2][:rows], start, 1)]
    reduce_scatter x1, waiting for transfers between devices: 12.9 us -> 33.4 us  [per_device(): gup = lax.psum_scatter(gup, 'uly', scatter_dimension=1, tiled=True)]
    all_to_all x1 -> x0, blocking collectives: 19.7 us -> none  [per_device(): lax.all_to_all(key_base, 'uly', split_axis=1, concat_axis=0, tiled=True)]
  transfers between devices with their start and end apart: 8 -> 3, of which waited for: 5 -> 3; matrix products, arithmetic and copies ran while one was open for 6% -> 1% of each run, Pallas kernels for 0% -> 0%
where the time goes in v1:
time: 354 us
  waiting for transfers between devices  246 us (69%)
  Pallas kernels  78.9 us (22%)
  between operations  15.5 us (4%)
  local copies, waits for them, and re-layouts  10.4 us (3%)
    psum x1, waiting for transfers between devices, per_device(): down_total = lax.psum(inner(tokens, lowrank).astype(BF16), ('blk', 'uly'))  122 us
    psum x1, waiting for transfers between devices, per_device(): gup = lax.psum(gup, 'blk')  91.3 us
    pallas_call x1, Pallas kernels, attention(): pl.pallas_call(functools.partial(attention_kernel, nb, nu), out_shape=(ja...  78.9 us
    reduce_scatter x1, waiting for transfers between devices, per_device(): gup = lax.psum_scatter(gup, 'uly', scatter_dimension=1, tiled=True)  33.4 us
  transfers between devices with their start and end apart: 3, of which 3 were waited for; matrix products, arithmetic and copies ran while one was open for 1% of the time, Pallas kernels for 0%

profile of v1, /device:TPU:0, one launch (start us, length us, event | category | flops | bytes accessed | tf_op | source)
XLA Modules:
  0.0 353.7 jit_solution(14252424424297351192)
XLA Ops:
  8.0 0.0 copy-start.2
  8.0 0.0 reduce-scatter.2.cloned.1.call-start
  8.1 2.4 copy.14.down_q
  10.4 0.0 copy-done.2
  10.4 1.4 copy.15.down_v
  11.8 78.9 %shard_map.128 = (bf16[128,5120]{1,0:T(8,128)(2,1)}, bf16[128,5120]{1,0:T(8,128)(2,1)}, bf16[128,128]{1,0:T(8,128)(2,1)}) custom-call(bf16[128,5120]{1,0:T(8,128)(2,1)} %tokens.1, bf16[128,5120]{1,0:T(8,128)(2,1)} %query_base.1, bf16[128,5120]{1,0:T(8,128)(2,1)} %key_base.1, bf16[128,5120]{1,0:T(8,128)(2,1)} %value_base.1, bf16[128,5120]{1,0:T(8,128)(2,1)} %out_grad.1, ...), custom_call_target="tpu_custom_call" | custom-call | tf_op jit(solution)/shard_map/pallas_call | solution.py:353
  90.7 0.0 copy-start
  90.8 0.0 reduce-scatter.2.cloned.1.call-update
  90.8 0.0 all-reduce.3.cloned.1.call-start
  90.8 1.2 copy-done
  92.1 2.3 fusion
  94.4 0.0 all-reduce.3.cloned.1.call-update
  94.4 0.0 all-reduce.5.cloned.1.call-start
  94.5 33.4 %reduce-scatter.2.cloned.1.call-done = bf16[128,2560]{1,0:T(8,128)(2,1)} async-done(((bf16[128,5120]{1,0:T(8,128)(2,1)}), bf16[128,2560]{1,0:T(8,128)(2,1)}) %reduce-scatter.2.cloned.1.call-update) | async-done | bytes 655376 | tf_op jit(solution)/shard_map/reduce_scatter | solution.py:393
  127.9 0.0 all-reduce.5.cloned.1.call-update
  127.9 121.7 %all-reduce.3.cloned.1.call-done = bf16[5120,128]{0,1:T(8,128)(2,1)} async-done(((bf16[5120,128]{0,1:T(8,128)(2,1)}), bf16[5120,128]{0,1:T(8,128)(2,1)}) %all-reduce.3.cloned.1.call-update) | async-done | bytes 1310736 | tf_op jit(solution)/shard_map/psum | solution.py:392
  249.6 2.4 fusion.1
  252.0 0.0 copy-start.1
  252.0 91.3 %all-reduce.5.cloned.1.call-done = bf16[128,2560]{1,0:T(8,128)(2,1)} async-done(((bf16[128,2560]{1,0:T(8,128)(2,1)}), bf16[128,2560]{1,0:T(8,128)(2,1)}) %all-reduce.5.cloned.1.call-update) | async-done | bytes 655376 | tf_op jit(solution)/shard_map/psum | solution.py:394
  343.3 1.9 fusion.2
  345.2 0.0 copy-done.1
  345.2 1.1 copy.19
Async XLA Ops:
  8.0 2.4 copy-start.2
  8.0 119.9 %reduce-scatter.2.cloned.1.call-start = ((), (), s32[]{:S(2)}) async-start(), calls=%async_computation.2 | async-start | bytes 1966080 | tf_op jit(solution)/shard_map/reduce_scatter | solution.py:393
  90.7 1.3 copy-start
  90.8 158.8 %all-reduce.3.cloned.1.call-start = ((), (), s32[]{:S(2)}) async-start(), calls=%async_computation.1 | async-start | bytes 2621440 | tf_op jit(solution)/shard_map/psum | solution.py:392
  94.4 248.8 %all-reduce.5.cloned.1.call-start = ((), (), s32[]{:S(2)}) async-start(), calls=%async_computation.3 | async-start | bytes 1310720 | tf_op jit(solution)/shard_map/psum | solution.py:394
  252.0 93.2 %copy-start.1 = (bf16[128,5120]{1,0:T(8,128)(2,1)S(1)}, bf16[128,5120]{1,0:T(8,128)(2,1)}, u32[]{:S(2)}) copy-start(bf16[128,5120]{1,0:T(8,128)(2,1)} %get-tuple-element.20) | copy-start | bytes 3932164
Sparse Core Ops, SparseCore 0:
  90.9 36.9 reduce-scatter.1
Sparse Core Ops, SparseCore 1:
  97.2 152.3 all-reduce.2
  252.8 90.4 all-reduce.4

commit v2 on v1

--- a/solution.py
+++ b/solution.py
@@ -240,7 +240,8 @@
         score_grad = (probs.astype(F32) * (outer(grad, values) - delta)).astype(BF16)
         query_grad = (dot(score_grad, keys) * scale).astype(BF16)
         seen = dot(probs, lbuf[...]).astype(BF16)
-        gup_ref[:, at] = (inner(low_qm, query_grad) + inner(seen, grad)).astype(BF16)
+        here = pl.ds(pl.multiple_of(h * 2 * rank, 2 * rank), 2 * rank)
+        gup_ref[here, :] = (inner(low_qm, query_grad) + inner(seen, grad)).astype(BF16)
         lrq[...] += jnp.where(lane < rank, outer(query_grad, up), 0.0)
         lifted = jnp.where(lane >= rank, outer(grad, up), 0.0).astype(BF16)
         lrv[...] += inner(probs, lifted)
@@ -354,7 +355,7 @@
         functools.partial(attention_kernel, nb, nu),
         out_shape=(
             jax.ShapeDtypeStruct((rows, width), BF16),
-            jax.ShapeDtypeStruct((2 * rank, width), BF16),
+            jax.ShapeDtypeStruct((width // HEAD * 2 * rank, HEAD), BF16),
             jax.ShapeDtypeStruct((rows, 2 * rank), BF16),
         ),
         in_specs=[anywhere] * 9,
@@ -384,21 +385,239 @@
     )(*operands)
 
 
+def reduction_kernel(
+    nb, nu,
+    tokens, lowrank, gup,
+    down_out, upq_out, upv_out,
+    tok, terms, pair, part, slots, down, ups, flat,
+    local_sem, psend, precv, ssend, srecv, bsend, brecv, csend, crecv,
+):
+    blk = lax.axis_index("blk")
+    u = lax.axis_index("uly")
+    core = lax.rem(blk, 2)
+    chip = blk // 2
+    other = chip * 2 + 1 - core
+    half = nb // 2
+    chips = half * nu
+    rows, width = tokens.shape
+    rank = upq_out.shape[0]
+    region = pair.shape[2]
+    piece = slots.shape[2]
+
+    def peer_u(o):
+        return lax.rem(u + o // half, nu)
+
+    def peer_chip(o):
+        return lax.rem(chip + lax.rem(o, half), half)
+
+    def from_u(o):
+        return lax.rem(u - o // half + nu, nu)
+
+    def from_chip(o):
+        return lax.rem(chip - lax.rem(o, half) + half, half)
+
+    def at(c):
+        return pl.ds(pl.multiple_of(c * piece, piece), piece)
+
+    barrier = pltpu.get_barrier_semaphore()
+    pl.semaphore_signal(barrier, inc=1, device_id=(other, u), device_id_type=MESH)
+
+    @pl.loop(1, chips)
+    def _(o):
+        pl.semaphore_signal(
+            barrier, inc=1, device_id=(peer_chip(o) * 2 + core, peer_u(o)), device_id_type=MESH
+        )
+
+    load = pltpu.make_async_copy(tokens, tok, local_sem.at[0])
+    load.start()
+    pl.semaphore_wait(barrier, chips)
+
+    def swap(t, v):
+        rows_at = pl.ds(pl.multiple_of((v * 2 + 1 - core) * region, region), region)
+        return pltpu.make_async_remote_copy(
+            src_ref=(terms if t == 0 else gup).at[rows_at], dst_ref=pair.at[t, v],
+            send_sem=psend.at[t, v], recv_sem=precv.at[t, v],
+            device_id=(other, u), device_id_type=MESH,
+        )
+
+    def scatter(t, o):
+        return pltpu.make_async_remote_copy(
+            src_ref=part.at[t, peer_u(o), at(peer_chip(o))], dst_ref=slots.at[t, o],
+            send_sem=ssend.at[t, o], recv_sem=srecv.at[t, o],
+            device_id=(peer_chip(o) * 2 + core, peer_u(o)), device_id_type=MESH,
+        )
+
+    def place(t, v, k, c):
+        return down.at[v, k, at(c)] if t == 0 else ups.at[k, at(c)]
+
+    def spread(t, o):
+        mine = place(t, u, core, chip)
+        return pltpu.make_async_remote_copy(
+            src_ref=mine, dst_ref=mine, send_sem=bsend.at[t, o], recv_sem=brecv.at[t, o],
+            device_id=(peer_chip(o) * 2 + core, peer_u(o)), device_id_type=MESH,
+        )
+
+    def landed(t, o):
+        here = place(t, from_u(o), core, from_chip(o))
+        return pltpu.make_async_remote_copy(
+            src_ref=here, dst_ref=here, send_sem=bsend.at[t, o], recv_sem=brecv.at[t, o],
+            device_id=(other, u), device_id_type=MESH,
+        )
+
+    def share(t, o):
+        here = place(t, from_u(o), core, from_chip(o))
+        return pltpu.make_async_remote_copy(
+            src_ref=here, dst_ref=here, send_sem=csend.at[t, o], recv_sem=crecv.at[t, o],
+            device_id=(other, u), device_id_type=MESH,
+        )
+
+    def shared(t, o):
+        here = place(t, from_u(o), 1 - core, from_chip(o))
+        return pltpu.make_async_remote_copy(
+            src_ref=here, dst_ref=here, send_sem=csend.at[t, o], recv_sem=crecv.at[t, o],
+            device_id=(other, u), device_id_type=MESH,
+        )
+
+    if part.shape[2] > region:
+        part[...] = jnp.zeros_like(part)
+    for v in range(nu):
+        swap(1, v).start()
+
+    load.wait()
+    step = min(CHUNK, width)
+
+    @pl.loop(0, width // step)
+    def _(c):
+        cols = pl.ds(pl.multiple_of(c * step, step), step)
+        terms[cols, :] = inner(tok[:, cols], lowrank[...]).astype(BF16)
+
+    def pair_sum(t):
+        for v in range(nu):
+            rows_at = pl.ds(pl.multiple_of((v * 2 + core) * region, region), region)
+            own = (terms if t == 0 else gup)[rows_at, :]
+            swap(t, v).wait_recv()
+            part[t, v, pl.ds(0, region), :] = (
+                own.astype(F32) + pair[t, v].astype(F32)
+            ).astype(BF16)
+
+    for v in range(nu):
+        swap(0, v).start()
+    for t in (1, 0):
+        pair_sum(t)
+
+        @pl.loop(1, chips)
+        def _(o):
+            scatter(t, o).start()
+
+    counts = (chips, half)
+    for t in (1, 0):
+
+        def add(o, total):
+            scatter(t, o).wait_recv()
+            return total + slots[t, o].astype(F32)
+
+        total = lax.fori_loop(1, chips, add, part[t, u, at(chip), :].astype(F32))
+        if t == 0:
+            down[u, core, at(chip), :] = total.astype(BF16)
+        else:
+            ups[core, at(chip), :] = total.astype(BF16)
+
+        @pl.loop(1, counts[t])
+        def _(o):
+            spread(t, o).start()
+
+        share(t, 0).start()
+
+    for t in (1, 0):
+
+        @pl.loop(1, counts[t])
+        def _(o):
+            landed(t, o).wait_recv()
+            share(t, o).start()
+
+    for t in (1, 0):
+
+        @pl.loop(0, counts[t])
+        def _(o):
+            shared(t, o).wait_recv()
+
+        if t == 1:
+            for k in range(2):
+                flat[pl.ds(k * region, region), :] = ups[k, pl.ds(0, region), :]
+            for h in range(2 * region // (2 * rank)):
+                cols = pl.ds(h * HEAD, HEAD)
+                upq_out[:, cols] = flat[pl.ds(h * 2 * rank, rank), :]
+                upv_out[:, cols] = flat[pl.ds(h * 2 * rank + rank, rank), :]
+        else:
+            for v in range(nu):
+                for k in range(2):
+                    down_out[pl.ds((v * 2 + k) * region, region), :] = down[
+                        v, k, pl.ds(0, region), :
+                    ]
+
+    for t in (1, 0):
+        for v in range(nu):
+            swap(t, v).wait_send()
+
+        @pl.loop(1, chips)
+        def _(o):
+            scatter(t, o).wait_send()
+
+        @pl.loop(1, counts[t])
+        def _(o):
+            spread(t, o).wait_send()
+
+        @pl.loop(0, counts[t])
+        def _(o):
+            share(t, o).wait_send()
+
+
+def reduction(nb, nu, tokens, lowrank, gup):
+    rows, width = tokens.shape
+    rank = lowrank.shape[1] // 2
+    half = nb // 2
+    chips = half * nu
+    region = width // (2 * nu)
+    piece = -(-region // (16 * half)) * 16
+    held = half * piece
+    dma = pltpu.SemaphoreType.DMA
+    here = pl.BlockSpec(memory_space=pltpu.VMEM)
+    lanes = lowrank.shape[1]
+    return pl.pallas_call(
+        functools.partial(reduction_kernel, nb, nu),
+        out_shape=(
+            jax.ShapeDtypeStruct((width, lanes), BF16),
+            jax.ShapeDtypeStruct((rank, width // nu), BF16),
+            jax.ShapeDtypeStruct((rank, width // nu), BF16),
+        ),
+        in_specs=[pl.BlockSpec(memory_space=pl.ANY), here, here],
+        out_specs=(here, here, here),
+        scratch_shapes=[
+            pltpu.VMEM((rows, width), BF16),
+            pltpu.VMEM((width, lanes), BF16),
+            pltpu.VMEM((2, nu, region, lanes), BF16),
+            pltpu.VMEM((2, nu, held, lanes), BF16),
+            pltpu.VMEM((2, chips, piece, lanes), BF16),
+            pltpu.VMEM((nu, 2, held, lanes), BF16),
+            pltpu.VMEM((2, held, lanes), BF16),
+            pltpu.VMEM((2 * region, lanes), BF16),
+            dma((1,)),
+            dma((2, nu)), dma((2, nu)),
+            dma((2, chips)), dma((2, chips)),
+            dma((2, chips)), dma((2, chips)),
+            dma((2, chips)), dma((2, chips)),
+        ],
+        compiler_params=pltpu.CompilerParams(collective_id=1, has_side_effects=True),
+    )(tokens, lowrank, gup)
+
+
 def per_device(nb, nu, tokens, query_base, key_base, value_base, out_grad, down_q, up_q, down_v, up_v):
     rank = down_q.shape[1]
     attended, gup, lowrank = attention(
         nb, nu, tokens, query_base, key_base, value_base, out_grad, down_q, up_q, down_v, up_v
     )
-    down_total = lax.psum(inner(tokens, lowrank).astype(BF16), ("blk", "uly"))
-    gup = lax.psum_scatter(gup, "uly", scatter_dimension=1, tiled=True)
-    gup = lax.psum(gup, "blk")
-    return (
-        attended,
-        down_total[:, :rank],
-        gup[:rank],
-        down_total[:, rank:],
-        gup[rank:],
-    )
+    down_total, grad_up_q, grad_up_v = reduction(nb, nu, tokens, lowrank, gup)
+    return attended, down_total[:, :rank], grad_up_q, down_total[:, rank:], grad_up_v
 
 
 def solution(mesh):

time: 354 us -> 166 us (0.47)
  waiting for transfers between devices: 246 us -> 0 us
  Pallas kernels: 78.9 us -> 154 us
  between operations: 15.5 us -> 0.67 us
    psum x2 -> x0, waiting for transfers between devices: 213 us -> none  [the longest x1 122 us: per_device(): down_total = lax.psum(inner(tokens, lowrank).astype(BF16), ('blk', 'uly'))]
    pallas_call x0 -> x1, Pallas kernels: none -> 74.8 us  [reduction(): pl.pallas_call(functools.partial(reduction_kernel, nb, nu), out_shape=(ja...]
    reduce_scatter x1 -> x0, waiting for transfers between devices: 33.4 us -> none  [per_device(): gup = lax.psum_scatter(gup, 'uly', scatter_dimension=1, tiled=True)]
    unnamed x9 -> x15, local copies, waits for them, and re-layouts: 6.07 us -> 9.12 us
  transfers between devices with their start and end apart: 3 -> 0, of which waited for: 3 -> 0; matrix products, arithmetic and copies ran while one was open for 1% -> 0% of each run, Pallas kernels for 0% -> 0%
where the time goes in v2:
time: 166 us
  Pallas kernels  154 us (93%)
  local copies, waits for them, and re-layouts  11.3 us (7%)
    pallas_call x1, Pallas kernels, attention(): pl.pallas_call(functools.partial(attention_kernel, nb, nu), out_shape=(ja...  78.9 us
    pallas_call x1, Pallas kernels, reduction(): pl.pallas_call(functools.partial(reduction_kernel, nb, nu), out_shape=(ja...  74.8 us
    unnamed x15, local copies, waits for them, and re-layouts  9.12 us

profile of v2, /device:TPU:0, one launch (start us, length us, event | category | flops | bytes accessed | tf_op | source)
XLA Modules:
  0.0 165.7 jit_solution(17029354591502284871)
XLA Ops:
  0.6 0.0 copy-start.1
  0.6 2.4 %copy.14.down_q = bf16[5120,64]{1,0:T(8,128)(2,1)} copy(bf16[5120,64]{0,1:T(8,128)(2,1)} %param.14) | data formatting | bytes 1310720 | tf_op args[5]
  3.0 0.0 copy-done.1
  3.0 1.4 copy.15.down_v
  4.4 78.9 %shard_map.128 = (bf16[128,5120]{1,0:T(8,128)(2,1)}, bf16[5120,128]{1,0:T(8,128)(2,1)}, bf16[128,128]{1,0:T(8,128)(2,1)}) custom-call(bf16[128,5120]{1,0:T(8,128)(2,1)} %tokens.3, bf16[128,5120]{1,0:T(8,128)(2,1)} %query_base.1, bf16[128,5120]{1,0:T(8,128)(2,1)} %key_base.1, bf16[128,5120]{1,0:T(8,128)(2,1)} %value_base.1, bf16[128,5120]{1,0:T(8,128)(2,1)} %out_grad.1, ...), custom_call_target="tpu_custom_call" | custom-call | tf_op jit(solution)/shard_map/pallas_call | solution.py:354
  83.3 74.8 %shard_map.129 = (bf16[5120,128]{1,0:T(8,128)(2,1)}, bf16[64,2560]{1,0:T(8,128)(2,1)}, bf16[64,2560]{1,0:T(8,128)(2,1)}) custom-call(bf16[128,5120]{1,0:T(8,128)(2,1)} %tokens.3, bf16[128,128]{1,0:T(8,128)(2,1)} %get-tuple-element.12.lowrank, bf16[5120,128]{1,0:T(8,128)(2,1)} %get-tuple-element.13.gup), custom_call_target="tpu_custom_call" | custom-call | tf_op jit(solution)/shard_map/pallas_call | solution.py:586
  158.2 2.2 %fusion = (bf16[5120,64]{1,0:T(8,128)(2,1)S(1)}, bf16[5120,64]{1,0:T(8,128)(2,1)S(1)}) fusion(bf16[5120,128]{1,0:T(8,128)(2,1)} %get-tuple-element.14), kind=kLoop, calls=%fused_computation | loop fusion | bytes 2621440 | tf_op jit(solution)/shard_map/slice | solution.py:620
  160.4 1.3 copy.17
  161.7 0.0 copy-start
  161.7 1.3 copy.16
  163.0 0.1 copy-done
  163.1 0.0 copy-start.3
  163.1 0.0 copy-start.2
  163.1 1.1 copy.21
  164.2 0.1 copy-done.3
  164.3 0.7 copy.22
  165.0 0.0 copy-done.2
  165.0 0.7 copy.23
Async XLA Ops:
  0.6 2.4 %copy-start.1 = (bf16[5120,64]{0,1:T(8,128)(2,1)S(1)}, bf16[5120,64]{0,1:T(8,128)(2,1)}, u32[]{:S(2)}) copy-start(bf16[5120,64]{0,1:T(8,128)(2,1)} %param.16) | copy-start | bytes 1966084
  161.7 1.4 copy-start
  163.1 1.2 copy-start.3
  163.1 1.9 %copy-start.2 = (bf16[64,2560]{1,0:T(8,128)(2,1)S(1)}, bf16[64,2560]{1,0:T(8,128)(2,1)}, u32[]{:S(2)}) copy-start(bf16[64,2560]{1,0:T(8,128)(2,1)} %get-tuple-element.33) | copy-start | bytes 983044

commit v3 on v1

--- a/solution.py
+++ b/solution.py
@@ -30,7 +30,7 @@
     nb, nu,
     tokens, query_base, key_base, value_base, out_grad, down_q, up_q, down_v, up_v,
     att_ref, gup_ref, low_out,
-    kbuf, vbuf, lbuf, tok, qs, gs, dq, dv, ups, lrq, lrv, lrin,
+    kbuf, vbuf, lbuf, tok, qs, gs, downs, ups, lrq, lrv, lrin,
     local_sem, xsend, xrecv, fsend, frecv, lsend, lrecv, msend, mrecv, rsend, rrecv,
 ):
     blk = lax.axis_index("blk")
@@ -70,7 +70,7 @@
         pltpu.make_async_copy(src, dst, local_sem.at[i])
         for i, (src, dst) in enumerate(
             (
-                (tokens, tok), (down_v, dv), (down_q, dq),
+                (tokens, tok), (down_q, downs.at[pl.ds(0, rank)]), (down_v, downs.at[pl.ds(rank, rank)]),
                 (up_q, ups.at[pl.ds(0, rank)]), (up_v, ups.at[pl.ds(rank, rank)]),
                 (value_base, vbuf.at[mine]), (key_base, kbuf.at[mine]),
                 (query_base, qs), (out_grad, gs),
@@ -170,7 +170,7 @@
     lane = lax.broadcasted_iota(jnp.int32, (rows, 2 * rank), 1)
     for i in range(3):
         local[i].wait()
-    low = jnp.concatenate([dot(tok[...], dq[...]), dot(tok[...], dv[...])], axis=1)
+    low = outer(tok[...], downs[...])
     low_qm = jnp.where(lane < rank, low, 0.0).astype(BF16)
     low_vm = jnp.where(lane >= rank, low, 0.0).astype(BF16)
     lbuf[mine, :] = low_vm
@@ -240,7 +240,8 @@
         score_grad = (probs.astype(F32) * (outer(grad, values) - delta)).astype(BF16)
         query_grad = (dot(score_grad, keys) * scale).astype(BF16)
         seen = dot(probs, lbuf[...]).astype(BF16)
-        gup_ref[:, at] = (inner(low_qm, query_grad) + inner(seen, grad)).astype(BF16)
+        here = pl.ds(pl.multiple_of(h * 2 * rank, 2 * rank), 2 * rank)
+        gup_ref[here, :] = (inner(low_qm, query_grad) + inner(seen, grad)).astype(BF16)
         lrq[...] += jnp.where(lane < rank, outer(query_grad, up), 0.0)
         lifted = jnp.where(lane >= rank, outer(grad, up), 0.0).astype(BF16)
         lrv[...] += inner(probs, lifted)
@@ -354,7 +355,7 @@
         functools.partial(attention_kernel, nb, nu),
         out_shape=(
             jax.ShapeDtypeStruct((rows, width), BF16),
-            jax.ShapeDtypeStruct((2 * rank, width), BF16),
+            jax.ShapeDtypeStruct((width // HEAD * 2 * rank, HEAD), BF16),
             jax.ShapeDtypeStruct((rows, 2 * rank), BF16),
         ),
         in_specs=[anywhere] * 9,
@@ -366,8 +367,7 @@
             pltpu.VMEM((rows, width), BF16),
             pltpu.VMEM((rows, width), BF16),
             pltpu.VMEM((rows, width), BF16),
-            pltpu.VMEM((width, rank), BF16),
-            pltpu.VMEM((width, rank), BF16),
+            pltpu.VMEM((2 * rank, width), BF16),
             pltpu.VMEM((2 * rank, width), BF16),
             pltpu.VMEM((rows, 2 * rank), F32),
             pltpu.VMEM((2 * span, 2 * rank), F32),
@@ -384,21 +384,263 @@
     )(*operands)
 
 
+def reduction_kernel(
+    nb, nu,
+    tokens, lowrank, gup,
+    downq_out, downv_out, upq_out, upv_out,
+    tok, terms, pair, part, plane_in, line, line_in, down, ups, flat,
+    local_sem, psend, precv, asend, arecv, bsend, brecv, csend, crecv, dsend, drecv, esend, erecv,
+):
+    blk = lax.axis_index("blk")
+    u = lax.axis_index("uly")
+    core = lax.rem(blk, 2)
+    chip = blk // 2
+    other = chip * 2 + 1 - core
+    half = nb // 2
+    inners = plane_in.shape[1] // nu
+    outers = half // inners
+    y = lax.rem(chip, inners)
+    z = chip // inners
+    group = nu * inners
+    rows, width = tokens.shape
+    rank = upq_out.shape[0]
+    region = pair.shape[2]
+    sub = plane_in.shape[2]
+    piece = line_in.shape[2]
+
+    def split(o, sign):
+        pu = lax.rem(u + sign * (o // inners) + nu, nu)
+        py = lax.rem(y + sign * lax.rem(o, inners) + inners, inners)
+        return pu, py
+
+    def plane_dev(o):
+        pu, py = split(o, 1)
+        return ((z * inners + py) * 2 + core, pu)
+
+    def peer_z(o):
+        return lax.rem(z + o, outers)
+
+    def from_z(o):
+        return lax.rem(z - o + outers, outers)
+
+    def line_dev(o):
+        return ((peer_z(o) * inners + y) * 2 + core, u)
+
+    def subs(p):
+        return pl.ds(pl.multiple_of(p * sub, sub), sub)
+
+    barrier = pltpu.get_barrier_semaphore()
+    pl.semaphore_signal(barrier, inc=1, device_id=(other, u), device_id_type=MESH)
+    for o in range(1, group):
+        pl.semaphore_signal(barrier, inc=1, device_id=plane_dev(o), device_id_type=MESH)
+    for o in range(1, outers):
+        pl.semaphore_signal(barrier, inc=1, device_id=line_dev(o), device_id_type=MESH)
+
+    load = pltpu.make_async_copy(tokens, tok, local_sem.at[0])
+    load.start()
+    pl.semaphore_wait(barrier, group + outers - 1)
+
+    def remote(src, dst, send, recv, device):
+        return pltpu.make_async_remote_copy(
+            src_ref=src, dst_ref=dst, send_sem=send, recv_sem=recv,
+            device_id=device, device_id_type=MESH,
+        )
+
+    def swap(t, v):
+        rows_at = pl.ds(pl.multiple_of((v * 2 + 1 - core) * region, region), region)
+        return remote(
+            (terms if t == 0 else gup).at[rows_at], pair.at[t, v],
+            psend.at[t, v], precv.at[t, v], (other, u),
+        )
+
+    def scatter(t, o):
+        pu, py = split(o, 1)
+        return remote(
+            part.at[t, pu, subs(py)], plane_in.at[t, o],
+            asend.at[t, o], arecv.at[t, o], plane_dev(o),
+        )
+
+    def pass_on(t, o):
+        at = pl.ds(pl.multiple_of(peer_z(o) * piece, piece), piece)
+        return remote(
+            line.at[t, at], line_in.at[t, o], bsend.at[t, o], brecv.at[t, o], line_dev(o)
+        )
+
+    def whole(t, v, k, p):
+        return down.at[v, k, subs(p)] if t == 0 else ups.at[k, subs(p)]
+
+    def piece_at(p, q):
+        return pl.ds(pl.multiple_of(p * sub + q * piece, piece), piece)
+
+    def small(t, q):
+        return down.at[u, core, piece_at(y, q)] if t == 0 else ups.at[core, piece_at(y, q)]
+
+    def along(t, o):
+        return remote(small(t, z), small(t, z), csend.at[t, o], crecv.at[t, o], line_dev(o))
+
+    def came(t, o):
+        here = small(t, from_z(o))
+        return remote(here, here, csend.at[t, o], crecv.at[t, o], line_dev(o))
+
+    def spread(t, o):
+        here = whole(t, u, core, y)
+        return remote(here, here, dsend.at[t, o], drecv.at[t, o], plane_dev(o))
+
+    def landed(t, o):
+        pu, py = split(o, -1)
+        here = whole(t, pu, core, py)
+        return remote(here, here, dsend.at[t, o], drecv.at[t, o], (other, u))
+
+    def share(t, o):
+        pu, py = split(o, -1)
+        here = whole(t, pu, core, py)
+        return remote(here, here, esend.at[t, o], erecv.at[t, o], (other, u))
+
+    def shared(t, o):
+        pu, py = split(o, -1)
+        here = whole(t, pu, 1 - core, py)
+        return remote(here, here, esend.at[t, o], erecv.at[t, o], (other, u))
+
+    if part.shape[2] > region:
+        part[...] = jnp.zeros_like(part)
+    for v in range(nu):
+        swap(1, v).start()
+
+    load.wait()
+    lows = lowrank[...]
+
+    @pl.loop(0, width // HEAD)
+    def _(h):
+        cols = pl.ds(pl.multiple_of(h * HEAD, HEAD), HEAD)
+        here = pl.ds(pl.multiple_of(h * 2 * rank, 2 * rank), 2 * rank)
+        terms[here, :] = inner(lows, tok[:, cols]).astype(BF16)
+
+    for v in range(nu):
+        swap(0, v).start()
+
+    for t in (1, 0):
+        for v in range(nu):
+            rows_at = pl.ds(pl.multiple_of((v * 2 + core) * region, region), region)
+            own = (terms if t == 0 else gup)[rows_at, :]
+            swap(t, v).wait_recv()
+            part[t, v, pl.ds(0, region), :] = (
+                own.astype(F32) + pair[t, v].astype(F32)
+            ).astype(BF16)
+        for o in range(1, group):
+            scatter(t, o).start()
+
+    for t in (1, 0):
+        total = part[t, u, subs(y), :].astype(F32)
+        for o in range(1, group):
+            scatter(t, o).wait_recv()
+            total = total + plane_in[t, o].astype(F32)
+        line[t, :, :] = total.astype(BF16)
+        for o in range(1, outers):
+            pass_on(t, o).start()
+
+    for t in (1, 0):
+        total = line[t, pl.ds(pl.multiple_of(z * piece, piece), piece), :].astype(F32)
+        for o in range(1, outers):
+            pass_on(t, o).wait_recv()
+            total = total + line_in[t, o].astype(F32)
+        small(t, z)[...] = total.astype(BF16)
+        for o in range(1, outers):
+            along(t, o).start()
+
+    counts = (group, inners)
+    for t in (1, 0):
+        for o in range(1, outers):
+            came(t, o).wait_recv()
+        for o in range(1, counts[t]):
+            spread(t, o).start()
+        share(t, 0).start()
+
+    for t in (1, 0):
+        for o in range(1, counts[t]):
+            landed(t, o).wait_recv()
+            share(t, o).start()
+
+    for t in (1, 0):
+        for o in range(counts[t]):
+            shared(t, o).wait_recv()
+        places = [(v, k) for v in range(nu if t == 0 else 1) for k in range(2)]
+        for n, (v, k) in enumerate(places):
+            flat[pl.ds(n * region, region), :] = (
+                down[v, k, pl.ds(0, region), :] if t == 0 else ups[k, pl.ds(0, region), :]
+            )
+        outs = (downq_out, downv_out) if t == 0 else (upq_out, upv_out)
+        for h in range(len(places) * region // (2 * rank)):
+            cols = pl.ds(h * HEAD, HEAD)
+            outs[0][:, cols] = flat[pl.ds(h * 2 * rank, rank), :]
+            outs[1][:, cols] = flat[pl.ds(h * 2 * rank + rank, rank), :]
+
+    for t in (1, 0):
+        for v in range(nu):
+            swap(t, v).wait_send()
+        for o in range(1, group):
+            scatter(t, o).wait_send()
+        for o in range(1, outers):
+            pass_on(t, o).wait_send()
+            along(t, o).wait_send()
+        for o in range(1, counts[t]):
+            spread(t, o).wait_send()
+        for o in range(counts[t]):
+            share(t, o).wait_send()
+
+
+def reduction(nb, nu, tokens, lowrank, gup):
+    rows, width = tokens.shape
+    rank = lowrank.shape[1] // 2
+    half = nb // 2
+    inners = 2 if half % 2 == 0 else 1
+    outers = half // inners
+    group = nu * inners
+    region = width // (2 * nu)
+    piece = -(-region // (16 * half)) * 16
+    sub = outers * piece
+    held = half * piece
+    dma = pltpu.SemaphoreType.DMA
+    here = pl.BlockSpec(memory_space=pltpu.VMEM)
+    lanes = lowrank.shape[1]
+    return pl.pallas_call(
+        functools.partial(reduction_kernel, nb, nu),
+        out_shape=(
+            jax.ShapeDtypeStruct((rank, width), BF16),
+            jax.ShapeDtypeStruct((rank, width), BF16),
+            jax.ShapeDtypeStruct((rank, width // nu), BF16),
+            jax.ShapeDtypeStruct((rank, width // nu), BF16),
+        ),
+        in_specs=[pl.BlockSpec(memory_space=pl.ANY), here, here],
+        out_specs=(here, here, here, here),
+        scratch_shapes=[
+            pltpu.VMEM((rows, width), BF16),
+            pltpu.VMEM((width, lanes), BF16),
+            pltpu.VMEM((2, nu, region, lanes), BF16),
+            pltpu.VMEM((2, nu, held, lanes), BF16),
+            pltpu.VMEM((2, group, sub, lanes), BF16),
+            pltpu.VMEM((2, sub, lanes), BF16),
+            pltpu.VMEM((2, outers, piece, lanes), BF16),
+            pltpu.VMEM((nu, 2, held, lanes), BF16),
+            pltpu.VMEM((2, held, lanes), BF16),
+            pltpu.VMEM((2 * nu * region, lanes), BF16),
+            dma((1,)),
+            dma((2, nu)), dma((2, nu)),
+            dma((2, group)), dma((2, group)),
+            dma((2, outers)), dma((2, outers)),
+            dma((2, outers)), dma((2, outers)),
+            dma((2, group)), dma((2, group)),
+            dma((2, group)), dma((2, group)),
+        ],
+        compiler_params=pltpu.CompilerParams(collective_id=1, has_side_effects=True),
+    )(tokens, lowrank, gup)
+
+
 def per_device(nb, nu, tokens, query_base, key_base, value_base, out_grad, down_q, up_q, down_v, up_v):
-    rank = down_q.shape[1]
     attended, gup, lowrank = attention(
-        nb, nu, tokens, query_base, key_base, value_base, out_grad, down_q, up_q, down_v, up_v
+        nb, nu, tokens, query_base, key_base, value_base, out_grad, down_q.T, up_q, down_v.T, up_v
     )
-    down_total = lax.psum(inner(tokens, lowrank).astype(BF16), ("blk", "uly"))
-    gup = lax.psum_scatter(gup, "uly", scatter_dimension=1, tiled=True)
-    gup = lax.psum(gup, "blk")
-    return (
-        attended,
-        down_total[:, :rank],
-        gup[:rank],
-        down_total[:, rank:],
-        gup[rank:],
-    )
+    grad_down_q, grad_down_v, grad_up_q, grad_up_v = reduction(nb, nu, tokens, lowrank, gup)
+    return attended, grad_down_q.T, grad_up_q, grad_down_v.T, grad_up_v
 
 
 def solution(mesh):

time: 354 us -> 152 us (0.43)
  waiting for transfers between devices: 246 us -> 0 us
  Pallas kernels: 78.9 us -> 145 us
  between operations: 15.5 us -> 0.68 us
  local copies, waits for them, and re-layouts: 10.4 us -> 4.96 us
    psum x2 -> x0, waiting for transfers between devices: 213 us -> none  [the longest x1 122 us: per_device(): down_total = lax.psum(inner(tokens, lowrank).astype(BF16), ('blk', 'uly'))]
    pallas_call x0 -> x1, Pallas kernels: none -> 66 us  [reduction(): pl.pallas_call(functools.partial(reduction_kernel, nb, nu), out_shape=(ja...]
    reduce_scatter x1 -> x0, waiting for transfers between devices: 33.4 us -> none  [per_device(): gup = lax.psum_scatter(gup, 'uly', scatter_dimension=1, tiled=True)]
    slice x2 -> x0, local copies, waits for them, and re-layouts: 4.37 us -> none  [the longest x1 2.42 us: per_device(): down_total[:, rank:]]
  transfers between devices with their start and end apart: 3 -> 0, of which waited for: 3 -> 0; matrix products, arithmetic and copies ran while one was open for 1% -> 0% of each run, Pallas kernels for 0% -> 0%
where the time goes in v3:
time: 152 us; the launch traced here: 151 us
  Pallas kernels  145 us (95%)
  local copies, waits for them, and re-layouts  4.96 us (3%)
    pallas_call x1, Pallas kernels, attention(): pl.pallas_call(functools.partial(attention_kernel, nb, nu), out_shape=(ja...  79 us
    pallas_call x1, Pallas kernels, reduction(): pl.pallas_call(functools.partial(reduction_kernel, nb, nu), out_shape=(ja...  66 us
    unnamed x15, local copies, waits for them, and re-layouts  4.96 us

profile of v3, /device:TPU:0, one launch (start us, length us, event | category | flops | bytes accessed | tf_op | source)
XLA Modules:
  0.0 150.7 jit_solution(11904591031809617826)
XLA Ops:
  0.6 79.0 %shard_map.128 = (bf16[128,5120]{1,0:T(8,128)(2,1)}, bf16[5120,128]{1,0:T(8,128)(2,1)}, bf16[128,128]{1,0:T(8,128)(2,1)}) custom-call(bf16[128,5120]{1,0:T(8,128)(2,1)} %tokens.3, bf16[128,5120]{1,0:T(8,128)(2,1)} %query_base.1, bf16[128,5120]{1,0:T(8,128)(2,1)} %key_base.1, bf16[128,5120]{1,0:T(8,128)(2,1)} %value_base.1, bf16[128,5120]{1,0:T(8,128)(2,1)} %out_grad.1, ...), custom_call_target="tpu_custom_call" | custom-call | tf_op jit(solution)/shard_map/pallas_call | solution.py:354
  79.6 0.0 copy-start
  79.6 66.0 %shard_map.129 = (bf16[64,5120]{1,0:T(8,128)(2,1)}, bf16[64,5120]{1,0:T(8,128)(2,1)}, bf16[64,2560]{1,0:T(8,128)(2,1)}, bf16[64,2560]{1,0:T(8,128)(2,1)}) custom-call(bf16[128,5120]{1,0:T(8,128)(2,1)} %tokens.3, bf16[128,128]{1,0:T(8,128)(2,1)} %get-tuple-element.13.lowrank, bf16[5120,128]{1,0:T(8,128)(2,1)} %get-tuple-element.14.gup), custom_call_target="tpu_custom_call" | custom-call | tf_op jit(solution)/shard_map/pallas_call | solution.py:605
  145.7 0.0 copy-done
  145.7 0.0 copy-start.2
  145.7 1.1 copy.19
  146.8 0.4 copy-done.2
  147.2 0.0 copy-start.4
  147.2 0.0 copy-start.1
  147.2 0.8 copy.20
  148.0 0.3 copy-done.4
  148.4 0.0 copy-start.3
  148.4 0.7 copy.21
  149.1 0.0 copy-done.1
  149.1 0.8 copy.22
  149.9 0.0 copy-done.3
  149.9 0.7 copy.23
Async XLA Ops:
  79.6 66.1 %copy-start = (bf16[128,5120]{1,0:T(8,128)(2,1)S(1)}, bf16[128,5120]{1,0:T(8,128)(2,1)}, u32[]{:S(2)}) copy-start(bf16[128,5120]{1,0:T(8,128)(2,1)} %get-tuple-element.24) | copy-start | bytes 3932164
  145.7 1.5 %copy-start.2 = (bf16[64,5120]{1,0:T(8,128)(2,1)S(1)}, bf16[64,5120]{1,0:T(8,128)(2,1)}, u32[]{:S(2)}) copy-start(bf16[64,5120]{1,0:T(8,128)(2,1)} %get-tuple-element.15) | copy-start | bytes 1966084
  147.2 1.2 copy-start.4
  147.2 1.9 %copy-start.1 = (bf16[64,5120]{1,0:T(8,128)(2,1)S(1)}, bf16[64,5120]{1,0:T(8,128)(2,1)}, u32[]{:S(2)}) copy-start(bf16[64,5120]{1,0:T(8,128)(2,1)} %get-tuple-element.17) | copy-start | bytes 1966084
  148.4 1.6 %copy-start.3 = (bf16[64,2560]{1,0:T(8,128)(2,1)S(1)}, bf16[64,2560]{1,0:T(8,128)(2,1)}, u32[]{:S(2)}) copy-start(bf16[64,2560]{1,0:T(8,128)(2,1)} %get-tuple-element.28) | copy-start | bytes 983044

commit v4 on v3

--- a/solution.py
+++ b/solution.py
@@ -235,16 +235,24 @@
         total = jnp.sum(weights, axis=1, keepdims=True)
         probs = (weights * (1.0 / total)).astype(BF16)
         attended = dot(probs, values).astype(BF16)
-        att_ref[:, at] = attended
         delta = jnp.sum(grad.astype(F32) * attended.astype(F32), axis=1, keepdims=True)
         score_grad = (probs.astype(F32) * (outer(grad, values) - delta)).astype(BF16)
         query_grad = (dot(score_grad, keys) * scale).astype(BF16)
         seen = dot(probs, lbuf[...]).astype(BF16)
-        here = pl.ds(pl.multiple_of(h * 2 * rank, 2 * rank), 2 * rank)
-        gup_ref[here, :] = (inner(low_qm, query_grad) + inner(seen, grad)).astype(BF16)
-        lrq[...] += jnp.where(lane < rank, outer(query_grad, up), 0.0)
+        gup = (inner(low_qm, query_grad) + inner(seen, grad)).astype(BF16)
         lifted = jnp.where(lane >= rank, outer(grad, up), 0.0).astype(BF16)
-        lrv[...] += inner(probs, lifted)
+        return attended, gup, outer(query_grad, up), inner(probs, lifted)
+
+    together = 2 if span <= 2 * HEAD else 1
+
+    def head_group(first):
+        results = [head(first + i) for i in range(together)]
+        for i, (attended, gup, _, _) in enumerate(results):
+            h = first + i
+            att_ref[:, pl.ds(pl.multiple_of(h * HEAD, HEAD), HEAD)] = attended
+            gup_ref[pl.ds(pl.multiple_of(h * 2 * rank, 2 * rank), 2 * rank), :] = gup
+        lrq[...] += jnp.where(lane < rank, sum(r[2] for r in results), 0.0)
+        lrv[...] += sum(r[3] for r in results)
 
     heads = CHUNK // HEAD
 
@@ -282,9 +290,9 @@
                     for j in range(nu):
                         arrived(a, j, c - 1).wait_recv()
 
-            @pl.loop(0, heads)
+            @pl.loop(0, heads // together)
             def _(i):
-                head((c - 1) * heads + i)
+                head_group((c - 1) * heads + i * together)
 
     def terms(k, j, base):
         s = peer(j)

time: 152 us -> 144 us (0.947)
  Pallas kernels: 145 us -> 138 us
    pallas_call x1, Pallas kernels: 66 us -> 60.3 us  [reduction(): pl.pallas_call(functools.partial(reduction_kernel, nb, nu), out_shape=(ja...]
where the time goes in v4:
time: 144 us
  Pallas kernels  138 us (96%)
  local copies, waits for them, and re-layouts  4.96 us (3%)
    pallas_call x1, Pallas kernels, attention(): pl.pallas_call(functools.partial(attention_kernel, nb, nu), out_shape=(ja...  77.6 us
    pallas_call x1, Pallas kernels, reduction(): pl.pallas_call(functools.partial(reduction_kernel, nb, nu), out_shape=(ja...  60.3 us
    unnamed x15, local copies, waits for them, and re-layouts  4.96 us

profile of v4, /device:TPU:0, one launch (start us, length us, event | category | flops | bytes accessed | tf_op | source)
XLA Modules:
  0.0 143.5 jit_solution(13349011079200315883)
XLA Ops:
  0.6 77.6 %shard_map.128 = (bf16[128,5120]{1,0:T(8,128)(2,1)}, bf16[5120,128]{1,0:T(8,128)(2,1)}, bf16[128,128]{1,0:T(8,128)(2,1)}) custom-call(bf16[128,5120]{1,0:T(8,128)(2,1)} %tokens.3, bf16[128,5120]{1,0:T(8,128)(2,1)} %query_base.1, bf16[128,5120]{1,0:T(8,128)(2,1)} %key_base.1, bf16[128,5120]{1,0:T(8,128)(2,1)} %value_base.1, bf16[128,5120]{1,0:T(8,128)(2,1)} %out_grad.1, ...), custom_call_target="tpu_custom_call" | custom-call | tf_op jit(solution)/shard_map/pallas_call | solution.py:362
  78.2 0.0 copy-start
  78.2 60.3 %shard_map.129 = (bf16[64,5120]{1,0:T(8,128)(2,1)}, bf16[64,5120]{1,0:T(8,128)(2,1)}, bf16[64,2560]{1,0:T(8,128)(2,1)}, bf16[64,2560]{1,0:T(8,128)(2,1)}) custom-call(bf16[128,5120]{1,0:T(8,128)(2,1)} %tokens.3, bf16[128,128]{1,0:T(8,128)(2,1)} %get-tuple-element.13.lowrank, bf16[5120,128]{1,0:T(8,128)(2,1)} %get-tuple-element.14.gup), custom_call_target="tpu_custom_call" | custom-call | tf_op jit(solution)/shard_map/pallas_call | solution.py:613
  138.5 0.0 copy-done
  138.5 0.0 copy-start.2
  138.6 1.1 copy.19
  139.6 0.4 copy-done.2
  140.1 0.0 copy-start.4
  140.1 0.0 copy-start.1
  140.1 0.8 copy.20
  140.9 0.3 copy-done.4
  141.2 0.0 copy-start.3
  141.2 0.7 copy.21
  141.9 0.0 copy-done.1
  142.0 0.8 copy.22
  142.8 0.0 copy-done.3
  142.8 0.7 copy.23
Async XLA Ops:
  78.2 60.3 %copy-start = (bf16[128,5120]{1,0:T(8,128)(2,1)S(1)}, bf16[128,5120]{1,0:T(8,128)(2,1)}, u32[]{:S(2)}) copy-start(bf16[128,5120]{1,0:T(8,128)(2,1)} %get-tuple-element.24) | copy-start | bytes 3932164
  138.5 1.5 %copy-start.2 = (bf16[64,5120]{1,0:T(8,128)(2,1)S(1)}, bf16[64,5120]{1,0:T(8,128)(2,1)}, u32[]{:S(2)}) copy-start(bf16[64,5120]{1,0:T(8,128)(2,1)} %get-tuple-element.15) | copy-start | bytes 1966084
  140.1 1.2 copy-start.4
  140.1 1.9 %copy-start.1 = (bf16[64,5120]{1,0:T(8,128)(2,1)S(1)}, bf16[64,5120]{1,0:T(8,128)(2,1)}, u32[]{:S(2)}) copy-start(bf16[64,5120]{1,0:T(8,128)(2,1)} %get-tuple-element.17) | copy-start | bytes 1966084
  141.2 1.6 %copy-start.3 = (bf16[64,2560]{1,0:T(8,128)(2,1)S(1)}, bf16[64,2560]{1,0:T(8,128)(2,1)}, u32[]{:S(2)}) copy-start(bf16[64,2560]{1,0:T(8,128)(2,1)} %get-tuple-element.28) | copy-start | bytes 983044
